TPU v7x, 32 devices: a whole 2x2x4 slice. The times are simulated.
32 devices in a mesh: dp: 8 (over y, x, core), exch: 4 (over z).
Axes of the slice: x: 2, y: 2, z: 4, core: 2. Of those that a mesh axis runs over, the one named last changes fastest.
Arguments:
- x_raw: bfloat16 [1024, 2048], P('exch', 'dp'), may hold values from -6 to 6
- bc_raw: bfloat16 [1024, 256], P(('exch', 'dp')), may hold values from -6 to 6
- dt_raw: bfloat16 [32, 1024], P('dp', 'exch'), may hold values from -4 to 4
- cotangent: bfloat16 [1024, 2048], P('exch', 'dp'), may hold values from -6 to 6
- ssm_state: bfloat16 [8, 32, 64, 128], P('exch', 'dp'), may hold values from -0.625 to 0.625
- conv_x_state: bfloat16 [8, 3, 2048], P('exch', None, 'dp'), may hold values from -6 to 6
- conv_bc_state: bfloat16 [8, 3, 256], P('exch'), may hold values from -6 to 6
- owner: int32 [8], P('exch'), may hold values from 0 to 3, as said below
- resp_len: int32 [8], P('exch'), may hold values from 32 to 128, as said below
- conv_x_weight: float32 [4, 2048], P(None, 'dp'), may hold values from -3 to 3
- conv_bc_weight: float32 [4, 256], replicated, may hold values from -3 to 3
- dt_bias: float32 [32], P('dp'), may hold values from -5 to -3
- a_log: float32 [32], P('dp'), may hold values from -2.3 to 2.1
- skip_d: float32 [32], P('dp'), may hold values from 0.5 to 1.5
Outputs:
- grad_x: bfloat16 [1024, 2048], P('exch', 'dp')
- grad_bc: bfloat16 [1024, 256], P(('exch', 'dp'))
- grad_dt: bfloat16 [32, 1024], P('dp', 'exch')
- grad_conv_x: float32 [4, 2048], P(None, 'dp')
- grad_conv_bc: float32 [4, 256], replicated
- grad_heads: float32 [3, 32], P(None, 'dp')
Inputs may be any that keep to these rules, and one draw needn't show every extreme that they name: `owner`: among the 2 prompts of one holder (an aligned block along exch) no learner index occurs more than 1 times, and some learner index occurs exactly 1 times; over all 8 prompts every learner index occurs exactly 2 times. `resp_len`: every learner's block of 2 responses holds a response of length 128.
All inputs are finite; a program needn't handle non-finite values.
Results may differ from a plain program's by a relative error of at most 0.001.
Values may be sent and summed in bfloat16 or wider, within the bound.
A program may use at most 64 MiB of HBM per device.

v0:
```python
import jax
import jax.numpy as jnp
from jax import lax
from jax.sharding import PartitionSpec as P

DEV_GROUP = 8
SPAN = 128
GROUP = 1
CAP = 1
PRECISE = lax.Precision.HIGHEST


def conv_pre(raw, state, weight):
    padded = jnp.concatenate([state, raw], axis=1)
    length = raw.shape[1]
    total = padded[:, 0:length] * weight[0]
    for offset in range(1, weight.shape[0]):
        total = total + padded[:, offset : offset + length] * weight[offset]
    return total


def ssd_output(values, proj_b, proj_c, steps, rate, skip, start, block):
    rows, length, heads, width = values.shape
    count = length // block
    value_blocks = values.reshape(rows, count, block, heads, width)
    b_blocks = proj_b.reshape(rows, count, block, proj_b.shape[-1])
    c_blocks = proj_c.reshape(rows, count, block, proj_c.shape[-1])
    step_blocks = steps.reshape(rows, count, block, heads)
    logs = jnp.cumsum(-rate * step_blocks, axis=2)
    causal = jnp.tril(jnp.ones((block, block), jnp.float32))
    spread = logs[:, :, :, None, :] - logs[:, :, None, :, :]
    decays = jnp.exp(jnp.where(causal[:, :, None] > 0.5, spread, 0.0)) * causal[:, :, None]
    scores = jnp.einsum("rntk,rnsk->rnts", c_blocks, b_blocks, precision=PRECISE)
    weighted = value_blocks * step_blocks[..., None]
    mixing = scores[..., None] * decays
    intra = jnp.einsum("rntsh,rnshp->rnthp", mixing, weighted, precision=PRECISE)
    entry = jnp.exp(logs[:, 0])
    carried = jnp.einsum("rtk,rhpk->rthp", c_blocks[:, 0], start, precision=PRECISE)
    pieces = [carried * entry[..., None]]
    inter = jnp.stack(pieces, axis=1)
    output = intra + inter + skip[:, None] * value_blocks
    return output.reshape(rows, length, heads, width)


def window_loss(
    x_rows,
    bc_act,
    dt_rows,
    x_weight,
    bias,
    decay_log,
    skip,
    x_prev,
    start,
    cotan,
    mask,
    heads,
    block,
):
    x_act = jax.nn.silu(conv_pre(x_rows, x_prev, x_weight))
    rows, length, channels = x_rows.shape
    values = x_act.reshape(rows, length, heads, channels // heads)
    half = bc_act.shape[-1] // 2
    steps = jax.nn.softplus(dt_rows + bias)
    output = ssd_output(
        values,
        bc_act[..., :half],
        bc_act[..., half:],
        steps,
        jnp.exp(decay_log),
        skip,
        start,
        block,
    )
    return jnp.sum(output.reshape(rows, length, channels) * cotan * mask[..., None])


def local(
    x_raw,
    bc_raw,
    dt_raw,
    cotangent,
    ssm_state,
    conv_x_state,
    conv_bc_state,
    owner,
    resp_len,
    conv_x_weight,
    conv_bc_weight,
    dt_bias,
    a_log,
    skip_d,
):
    peer_count = lax.axis_size("exch")
    slices = lax.axis_size("dp")
    prompts = owner.shape[0]
    responses = resp_len.shape[0]
    head_count = dt_raw.shape[0]
    tokens = x_raw.shape[0]
    channels = x_raw.shape[1]
    pair_width = 2 * ssm_state.shape[-1]
    conv_depth = conv_x_state.shape[1]
    length = tokens // responses
    row_count = bc_raw.shape[0]
    groups = bc_raw.shape[1] // pair_width
    my_group = lax.axis_index("dp") // DEV_GROUP
    targets = jnp.arange(peer_count, dtype=jnp.int32)
    match = (owner[:, None] == targets[None, :]).astype(jnp.int32)
    earlier = jnp.cumsum(match, axis=0) - match
    places = jnp.sum(earlier * match, axis=1)
    slot_ids = jnp.arange(CAP, dtype=jnp.int32)
    routing = (match[:, :, None] == 1) & (places[:, None, None] == slot_ids[None, None, :])
    routing = routing.reshape(prompts, peer_count * CAP).astype(jnp.bfloat16)

    def pack_slots(values):
        moved = jnp.dot(routing.T, values.reshape(prompts, -1), preferred_element_type=jnp.float32)
        return moved.astype(jnp.bfloat16).reshape(peer_count, CAP, -1)

    bc_state = lax.dynamic_slice_in_dim(conv_bc_state, my_group * pair_width, pair_width, 2)
    filled = jnp.sum(routing, axis=0).reshape(peer_count, CAP)
    got_ssm, got_x, got_bc, got_fill = (
        lax.all_to_all(pack_slots(ssm_state), "exch", split_axis=0, concat_axis=0, tiled=True),
        lax.all_to_all(pack_slots(conv_x_state), "exch", split_axis=0, concat_axis=0, tiled=True),
        lax.all_to_all(pack_slots(bc_state), "exch", split_axis=0, concat_axis=0, tiled=True),
        lax.all_to_all(filled, "exch", split_axis=0, concat_axis=0, tiled=True),
    )
    present = (got_fill.reshape(peer_count * CAP) > 0.5).astype(jnp.int32)
    position = jnp.cumsum(present) - 1
    owned_ids = jnp.arange(prompts, dtype=jnp.int32)
    select = ((present[None, :] == 1) & (position[None, :] == owned_ids[:, None])).astype(
        jnp.bfloat16
    )

    def unpack(values, shape):
        chosen = jnp.dot(
            select, values.reshape(peer_count * CAP, -1), preferred_element_type=jnp.float32
        )
        return jnp.repeat(chosen, GROUP, axis=0).reshape(shape)

    start_state = unpack(got_ssm, (responses, head_count, channels // head_count, -1))
    x_prev = unpack(got_x, (responses, conv_depth, channels))
    bc_prev = unpack(got_bc, (responses, conv_depth, pair_width))
    gathered = lax.all_gather(bc_raw, "dp", axis=0, tiled=True)
    bc_local = lax.dynamic_slice_in_dim(gathered, my_group * pair_width, pair_width, 1)
    x_rows = x_raw.astype(jnp.float32).reshape(responses, length, channels)
    bc_rows = bc_local.astype(jnp.float32).reshape(responses, length, pair_width)
    cot_rows = cotangent.astype(jnp.float32).reshape(responses, length, channels)
    dt_rows = dt_raw.astype(jnp.float32).T.reshape(responses, length, head_count)
    live_mask = (jnp.arange(length, dtype=jnp.int32)[None, :] < resp_len[:, None]).astype(
        jnp.float32
    )
    bc_weight = lax.dynamic_slice_in_dim(conv_bc_weight, my_group * pair_width, pair_width, 1)
    bc_pre = conv_pre(bc_rows, bc_prev, bc_weight)
    bc_act, silu_back = jax.vjp(jax.nn.silu, bc_pre)

    def local_loss(x_in, bc_in, dt_in, x_weight, bias, decay_log, skip):
        return window_loss(
            x_in,
            bc_in,
            dt_in,
            x_weight,
            bias,
            decay_log,
            skip,
            x_prev,
            start_state,
            cot_rows,
            live_mask,
            head_count,
            SPAN,
        )

    grad_xr, grad_bca, grad_dtr, grad_wx, grad_bias, grad_decay, grad_skip = jax.grad(
        local_loss, argnums=(0, 1, 2, 3, 4, 5, 6)
    )(x_rows, bc_act, dt_rows, conv_x_weight, dt_bias, a_log, skip_d)
    grad_pre = silu_back(grad_bca)[0]
    unused, conv_back = jax.vjp(
        lambda raw, weight: conv_pre(raw, bc_prev, weight), bc_rows, bc_weight
    )
    grad_raw, grad_wbc = conv_back(grad_pre)
    returned = lax.all_to_all(
        grad_raw.reshape(slices, row_count, pair_width),
        "dp",
        split_axis=0,
        concat_axis=0,
        tiled=True,
    )
    grad_share = jnp.sum(returned.reshape(groups, DEV_GROUP, row_count, pair_width), axis=1)
    grad_share = grad_share.transpose(1, 0, 2).reshape(row_count, groups * pair_width)
    empty_taps = jnp.zeros((conv_depth + 1, groups * pair_width), jnp.float32)
    grad_wx, grad_bias, grad_decay, grad_skip = lax.psum(
        (grad_wx, grad_bias, grad_decay, grad_skip), "exch"
    )
    placed = lax.dynamic_update_slice_in_dim(empty_taps, grad_wbc, my_group * pair_width, 1)
    grad_taps = lax.psum(placed, ("dp", "exch"))
    grad_x = grad_xr.reshape(tokens, channels).astype(jnp.bfloat16)
    grad_bc = grad_share.astype(jnp.bfloat16)
    grad_dt = grad_dtr.reshape(tokens, head_count).T.astype(jnp.bfloat16)
    grad_heads = jnp.stack([grad_bias, grad_decay, grad_skip])
    return (grad_x, grad_bc, grad_dt, grad_wx, grad_taps, grad_heads)


def solution(mesh):
    in_specs = (
        P("exch", "dp"),
        P(("exch", "dp"), None),
        P("dp", "exch"),
        P("exch", "dp"),
        P("exch", "dp", None, None),
        P("exch", None, "dp"),
        P("exch", None, None),
        P("exch"),
        P("exch"),
        P(None, "dp"),
        P(),
        P("dp"),
        P("dp"),
        P("dp"),
    )
    out_specs = (
        P("exch", "dp"),
        P(("exch", "dp"), None),
        P("dp", "exch"),
        P(None, "dp"),
        P(),
        P(None, "dp"),
    )
    return jax.shard_map(local, mesh=mesh, in_specs=in_specs, out_specs=out_specs, check_vma=False)
```

profile of v0, /device:TPU:0, one launch (start us, length us, event | category | flops | bytes accessed | tf_op | source)
XLA Modules:
  0.0 124.4 jit_solution(9123671219750444243)
XLA Ops:
  0.6 0.7 fusion.80
  2.3 0.7 copy.167
  3.0 6.3 %all-to-all-start = ((bf16[4,1,1]{2,1,0:T(2,128)(2,1)}), bf16[4,1,1]{2,1,0:T(2,128)(2,1)S(1)}, u32[]{:S(2)}, u32[]{:S(2)}) async-start(bf16[4,1,1]{2,1,0:T(2,128)(2,1)} %copy.167), calls=%async_computation | async-start | bytes 4096 | tf_op jit(solution)/shard_map/all_to_all | solution.py:125
  9.4 1.2 reshape.547
  12.8 0.7 copy-done.7
  14.2 0.7 reduce.16
  18.1 9.3 %all_gather.3 = bf16[256,256]{1,0:T(8,128)(2,1)S(1)} all-gather(bf16[32,256]{1,0:T(8,128)(2,1)S(1)} %copy-done.4), channel_id=1, replica_groups=mesh['dp'=8,'exch'=4] {'dp'}, dimensions={0}, use_global_device_ids=true | all-gather | bytes 147456 | tf_op jit(solution)/shard_map/all_gather | solution.py:143
  27.8 1.0 reduce.18
  28.8 1.0 reshape.555
  29.8 0.9 copy-done.2
  31.1 5.1 %all-to-all-start.1 = ((bf16[4,2,384]{2,1,0:T(2,128)(2,1)}), bf16[4,2,384]{2,1,0:T(2,128)(2,1)S(1)}, u32[]{:S(2)}, u32[]{:S(2)}) async-start(bf16[4,2,384]{2,1,0:T(2,128)(2,1)} %reshape.553), calls=%async_computation.1 | async-start | bytes 12288 | tf_op jit(solution)/shard_map/all_to_all | solution.py:124
  36.6 5.2 %all-to-all-done.1 = bf16[4,2,384]{2,1,0:T(2,128)(2,1)S(1)} async-done(((bf16[4,2,384]{2,1,0:T(2,128)(2,1)}), bf16[4,2,384]{2,1,0:T(2,128)(2,1)S(1)}, u32[]{:S(2)}, u32[]{:S(2)}) %all-to-all-start.1) | async-done | bytes 6176 | tf_op jit(solution)/shard_map/all_to_all | solution.py:124
  41.8 3.2 %all-to-all-start.2 = ((bf16[4,2,384]{2,1,0:T(2,128)(2,1)}), bf16[4,2,384]{2,1,0:T(2,128)(2,1)S(1)}, u32[]{:S(2)}, u32[]{:S(2)}) async-start(bf16[4,2,384]{2,1,0:T(2,128)(2,1)} %reshape.551), calls=%async_computation.2 | async-start | bytes 12288 | tf_op jit(solution)/shard_map/all_to_all | solution.py:123
  45.3 5.4 %all-to-all-done.2 = bf16[4,2,384]{2,1,0:T(2,128)(2,1)S(1)} async-done(((bf16[4,2,384]{2,1,0:T(2,128)(2,1)}), bf16[4,2,384]{2,1,0:T(2,128)(2,1)S(1)}, u32[]{:S(2)}, u32[]{:S(2)}) %all-to-all-start.2) | async-done | bytes 6176 | tf_op jit(solution)/shard_map/all_to_all | solution.py:123
  50.6 3.4 %all-to-all-start.3 = ((bf16[4,2,16384]{2,1,0:T(2,128)(2,1)}), bf16[4,2,16384]{2,1,0:T(2,128)(2,1)S(1)}, u32[]{:S(2)}, u32[]{:S(2)}) async-start(bf16[4,2,16384]{2,1,0:T(2,128)(2,1)} %reshape.555), calls=%async_computation.3 | async-start | bytes 524288 | tf_op jit(solution)/shard_map/all_to_all | solution.py:122
  55.3 1.3 %fusion.10 = (f32[2,128,4]{1,2,0:T(4,128)S(1)}, f32[2,128,4]{1,2,0:T(4,128)S(1)}, f32[2,128,128]{2,1,0:T(8,128)S(1)}) fusion(f32[2,128,128]{2,1,0:T(8,128)S(1)} %fusion.46, f32[128,128]{1,0:T(8,128)S(1)} %fusion.52, f32[2,128,4]{1,2,0:T(4,128)S(1)} %copy.171, pred[128,128]{1,0:T(8,128)(4,1)S(1)} %broadcast_compare_fusion, ...), kind=kOutput, calls=%fused_computation.27 | convolution fusion | flops 102201344 | bytes 885760 | tf_op jit(solution)/shard_map/transpose(jvp(rntsh,rnshp->rnthp))/dot_general | solution.py:36
  57.3 0.8 multiply_reduce_fusion.10
  59.0 0.7 fusion.19
  63.4 39.4 %psum.36 = f32[4,256]{1,0:T(4,128)} all-reduce(f32[4,256]{1,0:T(4,128)S(1)} %pad_add_fusion.6), channel_id=1, replica_groups=mesh['dp'=8,'exch'=4] {'dp','exch'}, use_global_device_ids=true, to_apply=%region_21.22 | all-reduce | flops 1024 | bytes 8192 | tf_op jit(solution)/shard_map/psum | solution.py:195
  102.9 2.2 %reduce_window_sum.46 = f32[2,1,128,4]{3,2,1,0:T(8,128)S(1)} reduce-window(f32[2,1,128,4]{3,2,1,0:T(8,128)S(1)} %bitcast_add_fusion, f32[]{:T(128)} %constant.56.clone.1), window={size=1x1x128x1 pad=0_0x0_0x0_127x0_0}, to_apply=%region_11.12 | reduce-window | flops 130048 | bytes 8196 | tf_op jit(solution)/shard_map/transpose(jvp(jit(cumsum)))/reduce_window_sum | solution.py:29
  105.2 0.8 multiply_reduce_fusion.11
  106.1 0.8 pad_add_fusion
  106.9 4.8 %all-to-all-start.4 = ((f32[8,32,256]{2,1,0:T(8,128)}), f32[8,32,256]{2,1,0:T(8,128)S(1)}, u32[]{:S(2)}, u32[]{:S(2)}) async-start(f32[8,32,256]{2,1,0:T(8,128)} %bitcast.44), calls=%async_computation.4 | async-start | bytes 524288 | tf_op jit(solution)/shard_map/all_to_all | solution.py:181
  111.9 11.3 %all-reduce.18 = (f32[4,256]{1,0:T(4,128)}, f32[1,4]{1,0:T(1,128)S(1)}, f32[1,4]{1,0:T(1,128)S(1)}, f32[1,4]{1,0:T(1,128)S(1)}) all-reduce(f32[4,256]{1,0:T(4,128)S(1)} %pad_add_fusion.7, f32[1,4]{1,0:T(1,128)S(1)} %bitcast.233, f32[1,4]{1,0:T(1,128)S(1)} %multiply_bitcast_fusion, ...), channel_id=1, replica_groups=mesh['dp'=8,'exch'=4] {'exch'}, use_global_device_ids=true, to_apply=%region_16.17 | all-reduce | flops 1036 | bytes 8288 | tf_op jit(solution)/shard_map/psum | solution.py:191
  (101 shorter events, 16.5 us)
Async XLA Ops:
  0.6 12.8 %copy-start = (bf16[2,3,256]{2,0,1:T(2,128)(2,1)S(1)}, bf16[2,3,256]{2,0,1:T(2,128)(2,1)}, u32[]{:S(2)}) copy-start(bf16[2,3,256]{2,0,1:T(2,128)(2,1)} %param.19) | copy-start | bytes 9220
  1.4 0.7 copy-start.8
  3.0 28.1 %all-to-all-start = ((bf16[4,1,1]{2,1,0:T(2,128)(2,1)}), bf16[4,1,1]{2,1,0:T(2,128)(2,1)S(1)}, u32[]{:S(2)}, u32[]{:S(2)}) async-start(bf16[4,1,1]{2,1,0:T(2,128)(2,1)} %copy.167), calls=%async_computation | async-start | bytes 4096 | tf_op jit(solution)/shard_map/all_to_all | solution.py:125
  9.4 1.2 copy-start.1
  10.6 0.7 copy-start.13
  10.7 0.7 copy-start.11
  11.3 0.7 copy-start.3
  11.3 0.7 copy-start.5
  12.1 0.7 copy-start.6
  12.8 0.7 copy-start.7
  14.8 0.7 copy-start.10
  17.3 0.7 copy-start.4
  18.0 9.4 %copy-start.9 = (bf16[2,4,64,128]{3,2,1,0:T(8,128)(2,1)S(1)}, bf16[2,4,64,128]{3,2,1,0:T(8,128)(2,1)}, u32[]{:S(2)}) copy-start(bf16[2,4,64,128]{3,2,1,0:T(8,128)(2,1)} %param.18) | copy-start | bytes 393220
  29.8 0.9 copy-start.2
  31.1 10.7 %all-to-all-start.1 = ((bf16[4,2,384]{2,1,0:T(2,128)(2,1)}), bf16[4,2,384]{2,1,0:T(2,128)(2,1)S(1)}, u32[]{:S(2)}, u32[]{:S(2)}) async-start(bf16[4,2,384]{2,1,0:T(2,128)(2,1)} %reshape.553), calls=%async_computation.1 | async-start | bytes 12288 | tf_op jit(solution)/shard_map/all_to_all | solution.py:124
  41.8 8.8 %all-to-all-start.2 = ((bf16[4,2,384]{2,1,0:T(2,128)(2,1)}), bf16[4,2,384]{2,1,0:T(2,128)(2,1)S(1)}, u32[]{:S(2)}, u32[]{:S(2)}) async-start(bf16[4,2,384]{2,1,0:T(2,128)(2,1)} %reshape.551), calls=%async_computation.2 | async-start | bytes 12288 | tf_op jit(solution)/shard_map/all_to_all | solution.py:123
  50.6 10.2 %all-to-all-start.3 = ((bf16[4,2,16384]{2,1,0:T(2,128)(2,1)}), bf16[4,2,16384]{2,1,0:T(2,128)(2,1)S(1)}, u32[]{:S(2)}, u32[]{:S(2)}) async-start(bf16[4,2,16384]{2,1,0:T(2,128)(2,1)} %reshape.555), calls=%async_computation.3 | async-start | bytes 524288 | tf_op jit(solution)/shard_map/all_to_all | solution.py:122
  56.6 0.7 copy-start.12
  106.9 16.9 %all-to-all-start.4 = ((f32[8,32,256]{2,1,0:T(8,128)}), f32[8,32,256]{2,1,0:T(8,128)S(1)}, u32[]{:S(2)}, u32[]{:S(2)}) async-start(f32[8,32,256]{2,1,0:T(8,128)} %bitcast.44), calls=%async_computation.4 | async-start | bytes 524288 | tf_op jit(solution)/shard_map/all_to_all | solution.py:181
where the time goes:
time: 125 us; the launch traced here: 124 us
  blocking collectives  60.1 us (48%)
  starting transfers between devices  22.9 us (18%)
  local copies, waits for them, and re-layouts  12.2 us (10%)
  other arithmetic  11.7 us (9%)
  waiting for transfers between devices  11.2 us (9%)
  matrix products  5.42 us (4%)
    psum x1, blocking collectives, local(): grad_taps = lax.psum(placed, ('dp', 'exch'))  39.4 us
    psum x1, blocking collectives, local(): lax.psum((grad_wx, grad_bias, grad_decay, grad_skip), 'exch')  11.3 us
    all_gather x1, blocking collectives, local(): gathered = lax.all_gather(bc_raw, 'dp', axis=0, tiled=True)  9.34 us
    unnamed x37, local copies, waits for them, and re-layouts  7.99 us
    all_to_all x1, starting transfers between devices, local(): lax.all_to_all(filled, 'exch', split_axis=0, concat_axis=0, tiled=True)  6.35 us
    all_to_all x1, waiting for transfers between devices, local(): lax.all_to_all(pack_slots(conv_x_state), 'exch', split_axis=0, concat_axi...  5.35 us
    all_to_all x1, waiting for transfers between devices, local(): lax.all_to_all(pack_slots(bc_state), 'exch', split_axis=0, concat_axis=0,...  5.23 us
    all_to_all x1, starting transfers between devices, local(): lax.all_to_all(pack_slots(bc_state), 'exch', split_axis=0, concat_axis=0,...  5.11 us
  transfers between devices with their start and end apart: 5, of which 3 were waited for; matrix products, arithmetic and copies ran while one was open for 12% of the time, Pallas kernels for 0%

commit v1 on v0

--- a/solution.py
+++ b/solution.py
@@ -192,7 +192,7 @@
         (grad_wx, grad_bias, grad_decay, grad_skip), "exch"
     )
     placed = lax.dynamic_update_slice_in_dim(empty_taps, grad_wbc, my_group * pair_width, 1)
-    grad_taps = lax.psum(placed, ("dp", "exch"))
+    grad_taps = jnp.sum(lax.all_gather(placed, ("dp", "exch")), axis=0)
     grad_x = grad_xr.reshape(tokens, channels).astype(jnp.bfloat16)
     grad_bc = grad_share.astype(jnp.bfloat16)
     grad_dt = grad_dtr.reshape(tokens, head_count).T.astype(jnp.bfloat16)

time: 125 us -> 150 us (1.20)
  blocking collectives: 60.1 us -> 85.2 us
    all_gather x0 -> x1, blocking collectives: none -> 66 us  [local(): grad_taps = jnp.sum(lax.all_gather(placed, ('dp', 'exch')), axis=0)]
    psum x1 -> x0, blocking collectives: 39.4 us -> none  [local(): grad_taps = lax.psum(placed, ('dp', 'exch'))]
  transfers between devices with their start and end apart: 5 -> 5, of which waited for: 3 -> 3; matrix products, arithmetic and copies ran while one was open for 12% -> 10% of each run, Pallas kernels for 0% -> 0%
where the time goes in v1:
time: 150 us; the launch traced here: 149 us
  blocking collectives  85.2 us (57%)
  starting transfers between devices  21.5 us (14%)
  other arithmetic  12.3 us (8%)
  local copies, waits for them, and re-layouts  12.2 us (8%)
  waiting for transfers between devices  11.2 us (7%)
  matrix products  5.42 us (4%)
    all_gather x1, blocking collectives, local(): grad_taps = jnp.sum(lax.all_gather(placed, ('dp', 'exch')), axis=0)  66 us
    psum x1, blocking collectives, local(): lax.psum((grad_wx, grad_bias, grad_decay, grad_skip), 'exch')  9.94 us
    all_gather x1, blocking collectives, local(): gathered = lax.all_gather(bc_raw, 'dp', axis=0, tiled=True)  9.34 us
    unnamed x37, local copies, waits for them, and re-layouts  7.99 us
    all_to_all x1, starting transfers between devices, local(): lax.all_to_all(filled, 'exch', split_axis=0, concat_axis=0, tiled=True)  6.35 us
    all_to_all x1, waiting for transfers between devices, local(): lax.all_to_all(pack_slots(conv_x_state), 'exch', split_axis=0, concat_axi...  5.35 us
    all_to_all x1, waiting for transfers between devices, local(): lax.all_to_all(pack_slots(bc_state), 'exch', split_axis=0, concat_axis=0,...  5.23 us
    all_to_all x1, starting transfers between devices, local(): lax.all_to_all(pack_slots(bc_state), 'exch', split_axis=0, concat_axis=0,...  5.11 us
  transfers between devices with their start and end apart: 5, of which 3 were waited for; matrix products, arithmetic and copies ran while one was open for 10% of the time, Pallas kernels for 0%

profile of v1, /device:TPU:0, one launch (start us, length us, event | category | flops | bytes accessed | tf_op | source)
XLA Modules:
  0.0 148.9 jit_solution(10071724500012700689)
XLA Ops:
  0.6 0.7 fusion.80
  2.3 0.7 copy.167
  3.0 6.3 %all-to-all-start = ((bf16[4,1,1]{2,1,0:T(2,128)(2,1)}), bf16[4,1,1]{2,1,0:T(2,128)(2,1)S(1)}, u32[]{:S(2)}, u32[]{:S(2)}) async-start(bf16[4,1,1]{2,1,0:T(2,128)(2,1)} %copy.167), calls=%async_computation | async-start | bytes 4096 | tf_op jit(solution)/shard_map/all_to_all | solution.py:125
  9.4 1.2 reshape.551
  12.8 0.7 copy-done.7
  14.2 0.7 reduce.17
  18.1 9.3 %all_gather.9 = bf16[256,256]{1,0:T(8,128)(2,1)S(1)} all-gather(bf16[32,256]{1,0:T(8,128)(2,1)S(1)} %copy-done.4), channel_id=1, replica_groups=mesh['dp'=8,'exch'=4] {'dp'}, dimensions={0}, use_global_device_ids=true | all-gather | bytes 147456 | tf_op jit(solution)/shard_map/all_gather | solution.py:143
  27.8 1.0 reduce.19
  28.8 1.0 reshape.559
  29.8 0.9 copy-done.2
  31.1 5.1 %all-to-all-start.1 = ((bf16[4,2,384]{2,1,0:T(2,128)(2,1)}), bf16[4,2,384]{2,1,0:T(2,128)(2,1)S(1)}, u32[]{:S(2)}, u32[]{:S(2)}) async-start(bf16[4,2,384]{2,1,0:T(2,128)(2,1)} %reshape.557), calls=%async_computation.1 | async-start | bytes 12288 | tf_op jit(solution)/shard_map/all_to_all | solution.py:124
  36.6 5.2 %all-to-all-done.1 = bf16[4,2,384]{2,1,0:T(2,128)(2,1)S(1)} async-done(((bf16[4,2,384]{2,1,0:T(2,128)(2,1)}), bf16[4,2,384]{2,1,0:T(2,128)(2,1)S(1)}, u32[]{:S(2)}, u32[]{:S(2)}) %all-to-all-start.1) | async-done | bytes 6176 | tf_op jit(solution)/shard_map/all_to_all | solution.py:124
  41.8 3.2 %all-to-all-start.2 = ((bf16[4,2,384]{2,1,0:T(2,128)(2,1)}), bf16[4,2,384]{2,1,0:T(2,128)(2,1)S(1)}, u32[]{:S(2)}, u32[]{:S(2)}) async-start(bf16[4,2,384]{2,1,0:T(2,128)(2,1)} %reshape.555), calls=%async_computation.2 | async-start | bytes 12288 | tf_op jit(solution)/shard_map/all_to_all | solution.py:123
  45.3 5.4 %all-to-all-done.2 = bf16[4,2,384]{2,1,0:T(2,128)(2,1)S(1)} async-done(((bf16[4,2,384]{2,1,0:T(2,128)(2,1)}), bf16[4,2,384]{2,1,0:T(2,128)(2,1)S(1)}, u32[]{:S(2)}, u32[]{:S(2)}) %all-to-all-start.2) | async-done | bytes 6176 | tf_op jit(solution)/shard_map/all_to_all | solution.py:123
  50.6 3.4 %all-to-all-start.3 = ((bf16[4,2,16384]{2,1,0:T(2,128)(2,1)}), bf16[4,2,16384]{2,1,0:T(2,128)(2,1)S(1)}, u32[]{:S(2)}, u32[]{:S(2)}) async-start(bf16[4,2,16384]{2,1,0:T(2,128)(2,1)} %reshape.559), calls=%async_computation.3 | async-start | bytes 524288 | tf_op jit(solution)/shard_map/all_to_all | solution.py:122
  55.3 1.3 fusion.10
  57.3 0.8 multiply_reduce_fusion.10
  59.0 0.7 fusion.19
  63.4 66.0 %all-gather.1 = f32[32,4,256]{2,1,0:T(4,128)S(1)} all-gather(f32[1,4,256]{2,1,0:T(4,128)S(1)} %add_bitcast_fusion), channel_id=2, replica_groups=mesh['dp'=8,'exch'=4] {'dp','exch'}, dimensions={0}, use_global_device_ids=true | all-gather | bytes 135168 | tf_op jit(solution)/shard_map/all_gather | solution.py:195
  130.1 2.2 %reduce_window_sum.46 = f32[2,1,128,4]{3,2,1,0:T(8,128)S(1)} reduce-window(f32[2,1,128,4]{3,2,1,0:T(8,128)S(1)} %bitcast_add_fusion, f32[]{:T(128)} %constant.56.clone.1), window={size=1x1x128x1 pad=0_0x0_0x0_127x0_0}, to_apply=%region_11.12 | reduce-window | flops 130048 | bytes 8196 | tf_op jit(solution)/shard_map/transpose(jvp(jit(cumsum)))/reduce_window_sum | solution.py:29
  132.4 0.8 multiply_reduce_fusion.11
  133.3 0.8 pad_add_fusion
  134.1 3.4 %all-to-all-start.4 = ((f32[8,32,256]{2,1,0:T(8,128)}), f32[8,32,256]{2,1,0:T(8,128)S(1)}, u32[]{:S(2)}, u32[]{:S(2)}) async-start(f32[8,32,256]{2,1,0:T(8,128)} %bitcast.44), calls=%async_computation.4 | async-start | bytes 524288 | tf_op jit(solution)/shard_map/all_to_all | solution.py:181
  137.7 9.9 %all-reduce.18 = (f32[4,256]{1,0:T(4,128)}, f32[1,4]{1,0:T(1,128)S(1)}, f32[1,4]{1,0:T(1,128)S(1)}, f32[1,4]{1,0:T(1,128)S(1)}) all-reduce(f32[4,256]{1,0:T(4,128)S(1)} %pad_add_fusion.6, f32[1,4]{1,0:T(1,128)S(1)} %bitcast.235, f32[1,4]{1,0:T(1,128)S(1)} %multiply_bitcast_fusion, ...), channel_id=1, replica_groups=mesh['dp'=8,'exch'=4] {'exch'}, use_global_device_ids=true, to_apply=%region_16.17 | all-reduce | flops 1036 | bytes 8288 | tf_op jit(solution)/shard_map/psum | solution.py:191
  (102 shorter events, 17.1 us)
Async XLA Ops:
  0.6 12.8 %copy-start = (bf16[2,3,256]{2,0,1:T(2,128)(2,1)S(1)}, bf16[2,3,256]{2,0,1:T(2,128)(2,1)}, u32[]{:S(2)}) copy-start(bf16[2,3,256]{2,0,1:T(2,128)(2,1)} %param.19) | copy-start | bytes 9220
  1.4 0.7 copy-start.8
  3.0 28.1 %all-to-all-start = ((bf16[4,1,1]{2,1,0:T(2,128)(2,1)}), bf16[4,1,1]{2,1,0:T(2,128)(2,1)S(1)}, u32[]{:S(2)}, u32[]{:S(2)}) async-start(bf16[4,1,1]{2,1,0:T(2,128)(2,1)} %copy.167), calls=%async_computation | async-start | bytes 4096 | tf_op jit(solution)/shard_map/all_to_all | solution.py:125
  9.4 1.2 copy-start.1
  10.6 0.7 copy-start.13
  10.7 0.7 copy-start.11
  11.3 0.7 copy-start.3
  11.3 0.7 copy-start.5
  12.1 0.7 copy-start.6
  12.8 0.7 copy-start.7
  14.8 0.7 copy-start.10
  17.3 0.7 copy-start.4
  18.0 9.4 %copy-start.9 = (bf16[2,4,64,128]{3,2,1,0:T(8,128)(2,1)S(1)}, bf16[2,4,64,128]{3,2,1,0:T(8,128)(2,1)}, u32[]{:S(2)}) copy-start(bf16[2,4,64,128]{3,2,1,0:T(8,128)(2,1)} %param.18) | copy-start | bytes 393220
  29.8 0.9 copy-start.2
  31.1 10.7 %all-to-all-start.1 = ((bf16[4,2,384]{2,1,0:T(2,128)(2,1)}), bf16[4,2,384]{2,1,0:T(2,128)(2,1)S(1)}, u32[]{:S(2)}, u32[]{:S(2)}) async-start(bf16[4,2,384]{2,1,0:T(2,128)(2,1)} %reshape.557), calls=%async_computation.1 | async-start | bytes 12288 | tf_op jit(solution)/shard_map/all_to_all | solution.py:124
  41.8 8.8 %all-to-all-start.2 = ((bf16[4,2,384]{2,1,0:T(2,128)(2,1)}), bf16[4,2,384]{2,1,0:T(2,128)(2,1)S(1)}, u32[]{:S(2)}, u32[]{:S(2)}) async-start(bf16[4,2,384]{2,1,0:T(2,128)(2,1)} %reshape.555), calls=%async_computation.2 | async-start | bytes 12288 | tf_op jit(solution)/shard_map/all_to_all | solution.py:123
  50.6 10.2 %all-to-all-start.3 = ((bf16[4,2,16384]{2,1,0:T(2,128)(2,1)}), bf16[4,2,16384]{2,1,0:T(2,128)(2,1)S(1)}, u32[]{:S(2)}, u32[]{:S(2)}) async-start(bf16[4,2,16384]{2,1,0:T(2,128)(2,1)} %reshape.559), calls=%async_computation.3 | async-start | bytes 524288 | tf_op jit(solution)/shard_map/all_to_all | solution.py:122
  56.6 0.7 copy-start.12
  134.1 14.1 %all-to-all-start.4 = ((f32[8,32,256]{2,1,0:T(8,128)}), f32[8,32,256]{2,1,0:T(8,128)S(1)}, u32[]{:S(2)}, u32[]{:S(2)}) async-start(f32[8,32,256]{2,1,0:T(8,128)} %bitcast.44), calls=%async_computation.4 | async-start | bytes 524288 | tf_op jit(solution)/shard_map/all_to_all | solution.py:181
